TPU v7x, 32 devices: a whole 2x2x4 slice. The times are simulated.
32 devices in a mesh: row: 2 (over core), blk: 16 (over z, y, x).
Axes of the slice: x: 2, y: 2, z: 4, core: 2. Of those that a mesh axis runs over, the one named last changes fastest.
Arguments:
- state: float32 [2, 9, 5, 16, 2048], P('row', None, None, None, 'blk'), may hold values from -6 to 6
- inflow: float32 [9, 5, 2048], P(None, None, 'blk'), may hold values from -6 to 6
- blade_counts: int32 [2], replicated, may hold values from 20 to 60
- modes: int32 [1, 4], replicated, may hold values from 1 to 40
Outputs:
- advanced: float32 [2, 9, 5, 16, 2048], P('row', None, None, None, 'blk')
All inputs are finite; a program needn't handle non-finite values.
Results may differ from a plain program's by a relative error of at most 0.0001.
Values sent between devices are 32-bit elements; how exact they have to be, the bound alone decides.
A program may use at most 64 MiB of HBM per device.

v0:
```python
import math

import jax
import jax.numpy as jnp
from jax import lax
from jax.sharding import PartitionSpec as P

DIFFUSE = 0.05
FOURTH_SMOOTH = 0.03
COURANT = 0.6
FREQ_SCALE = 0.02


def from_behind(shard, axis, by):
    peers = lax.axis_size(axis)
    pairs = [(i, i + by) for i in range(peers) if 0 <= i + by < peers]
    return lax.ppermute(shard, axis, pairs)


def with_halo(shard, sides, width):
    for axis, dim in sides:
        peers, length = (lax.axis_size(axis), shard.shape[dim])
        up = [(i, (i + 1) % peers) for i in range(peers)]
        down = [(j, i) for i, j in up]
        last = lax.slice_in_dim(shard, length - width, length, axis=dim)
        leading = lax.slice_in_dim(shard, 0, width, axis=dim)
        before = lax.ppermute(last, axis, up)
        after = lax.ppermute(leading, axis, down)
        shard = jnp.concatenate([before, shard, after], axis=dim)
    return shard


def residual(padded, frequency):
    inner_depth = padded.shape[2] - 4
    inner_width = padded.shape[3] - 4

    def window_at(source, shift_j, shift_t):
        return source[
            :, :, 2 + shift_j : 2 + shift_j + inner_depth, 2 + shift_t : 2 + shift_t + inner_width
        ]

    steady = padded[0]
    speed_axial = 1.0 + 0.5 * jnp.tanh(steady[1])
    speed_turn = 0.5 * jnp.tanh(steady[2])
    cosines = padded[1::2]
    sines = padded[2::2]
    stress = 0.5 * jnp.sum(cosines[:, 1:2] * cosines + sines[:, 1:2] * sines, axis=0)
    flux_axial = speed_axial * padded + jnp.concatenate(
        [stress[None], jnp.zeros_like(padded[1:])], axis=0
    )
    flux_turn = speed_turn * padded
    center = window_at(padded, 0, 0)
    neighbours = (
        window_at(padded, 1, 0)
        + window_at(padded, -1, 0)
        + window_at(padded, 0, 1)
        + window_at(padded, 0, -1)
    )
    farther = (
        window_at(padded, 2, 0)
        + window_at(padded, -2, 0)
        + window_at(padded, 0, 2)
        + window_at(padded, 0, -2)
    )
    convect = -0.5 * (window_at(flux_axial, 1, 0) - window_at(flux_axial, -1, 0)) - 0.5 * (
        window_at(flux_turn, 0, 1) - window_at(flux_turn, 0, -1)
    )
    second = neighbours - 4.0 * center
    fourth = farther - 4.0 * neighbours + 12.0 * center
    rates = frequency[:, None, None, None]
    source_real = rates * center[2::2]
    source_imag = -rates * center[1::2]
    paired = jnp.stack([source_real, source_imag], axis=1).reshape((-1,) + center.shape[1:])
    source = jnp.concatenate([jnp.zeros_like(center[0:1]), paired], axis=0)
    return convect + DIFFUSE * second - FOURTH_SMOOTH * fourth + source


def local_step(field):
    steady = field[0]
    return COURANT / (1.0 + 0.5 * jnp.tanh(steady[1]) + jnp.abs(0.5 * jnp.tanh(steady[2])))


def rotate_modes(planes, table, sign, columns, total):
    pieces = [planes[0]]
    for harmonic in range(planes.shape[0] // 2):
        turns = jnp.remainder(table[harmonic] * columns, total)
        angle = 2.0 * math.pi / total * turns.astype(jnp.float32)
        cosine = jnp.cos(angle)
        sine = sign * jnp.sin(angle)
        real_part = planes[1 + 2 * harmonic]
        imag_part = planes[2 + 2 * harmonic]
        pieces.append(real_part * cosine - imag_part * sine)
        pieces.append(real_part * sine + imag_part * cosine)
    return jnp.stack(pieces)


def pad_columns(planes):
    return jnp.pad(planes, ((0, 0), (0, 0), (0, 0), (2, 2)))


def pick_row(table, wanted):
    chosen = jnp.arange(table.shape[0], dtype=jnp.int32)[:, None] == wanted
    return jnp.sum(jnp.where(chosen, table, 0), axis=0)


def pick_count(table, wanted):
    chosen = jnp.arange(table.shape[0], dtype=jnp.int32) == wanted
    return jnp.sum(jnp.where(chosen, table, 0))


def body(state, inflow, blade_counts, modes):
    start_state = state[0]
    depth = start_state.shape[2]
    width = start_state.shape[3]
    row_index = lax.axis_index("row")
    row_count = lax.axis_size("row")
    block_index = lax.axis_index("blk")
    total = width * lax.axis_size("blk")
    harmonics = (start_state.shape[0] - 1) // 2
    orders = jnp.arange(1, harmonics + 1, dtype=jnp.float32)
    frequency = FREQ_SCALE * pick_count(blade_counts, row_index).astype(jnp.float32) * orders
    upstream_modes = pick_row(modes, row_index - 1)
    downstream_modes = pick_row(modes, row_index)
    inflow_plane = inflow[:, :, None, :]
    own_columns = block_index * width + jnp.arange(width, dtype=jnp.int32)
    step_size = local_step(start_state)
    current = start_state
    for weight in (0.5, 1.0):
        outlet = from_behind(current[:, :, depth - 2 :, :], "row", 1)
        inlet = from_behind(current[:, :, :2, :], "row", -1)
        lower = jnp.where(
            row_index == 0,
            inflow_plane,
            rotate_modes(outlet, upstream_modes, 1.0, own_columns, total),
        )
        last_plane = current[:, :, depth - 1 :, :]
        upper = jnp.where(
            row_index == row_count - 1,
            jnp.concatenate([last_plane, last_plane], axis=2),
            rotate_modes(inlet, downstream_modes, -1.0, own_columns, total),
        )
        lower, upper = (pad_columns(lower), pad_columns(upper))
        extended = with_halo(current, (("blk", 3),), 2)
        padded = jnp.concatenate([lower, extended, upper], axis=2)
        current = start_state + weight * step_size * residual(padded, frequency)
    return current[None]


def solution(mesh):
    placed = (P("row", None, None, None, "blk"), P(None, None, "blk"), P(), P())
    return jax.shard_map(
        body,
        mesh=mesh,
        in_specs=placed,
        out_specs=P("row", None, None, None, "blk"),
        check_vma=False,
    )
```

profile of v0, /device:TPU:0, one launch (start us, length us, event | category | flops | bytes accessed | tf_op | source)
XLA Modules:
  0.0 58.3 jit_solution(11150004019017422067)
XLA Ops:
  0.0 0.0 copy-start
  0.0 0.0 copy-start.2
  0.0 0.0 copy-start.3
  0.0 1.1 %fusion.89 = (f32[9,5,2,128]{3,2,1,0:T(2,128)S(1)}, f32[9,5,2,128]{3,2,1,0:T(2,128)S(1)}) fusion(f32[9,5,16,128]{3,2,1,0:T(8,128)} %bitcast.45), kind=kLoop, calls=%fused_computation.218 | loop fusion | bytes 184320 | tf_op jit(solution)/shard_map/slice | solution.py:130
  1.1 1.3 %collective-permute-start.3 = (f32[9,5,2,128]{3,2,1,0:T(2,128)S(1)}, f32[9,5,2,128]{3,2,1,0:T(2,128)S(1)}, u32[]{:S(2)}, u32[]{:S(2)}) collective-permute-start(f32[9,5,2,128]{3,2,1,0:T(2,128)S(1)} %get-tuple-element.27), channel_id=1, source_target_pairs={{16,0},{17,1},{18,2},{19,3},{20,4},{21,5},{22,6},{23,7},{24,8},{25... | collective-permute-start | bytes 138248 | tf_op jit(solution)/shard_map/ppermute | solution.py:17
  2.4 3.0 %collective-permute-start = (f32[9,5,2,128]{3,2,1,0:T(2,128)S(1)}, f32[9,5,2,128]{3,2,1,0:T(2,128)S(1)}, u32[]{:S(2)}, u32[]{:S(2)}) collective-permute-start(f32[9,5,2,128]{3,2,1,0:T(2,128)S(1)} %get-tuple-element.28), channel_id=1, source_target_pairs={{0,16},{1,17},{2,18},{3,19},{4,20},{5,21},{6,22},{7,23},{8,24},{9,... | collective-permute-start | bytes 138248 | tf_op jit(solution)/shard_map/ppermute | solution.py:17
  5.5 1.3 %fusion.90 = (f32[9,5,16,2]{3,2,1,0:T(8,128)S(1)}, f32[9,5,16,2]{3,2,1,0:T(8,128)S(1)}) fusion(f32[9,5,16,128]{3,2,1,0:T(8,128)} %bitcast.46), kind=kLoop, calls=%fused_computation.219 | loop fusion | bytes 23040 | tf_op jit(solution)/shard_map/slice | solution.py:26
  6.7 7.0 %collective-permute-start.2 = (f32[9,5,16,2]{3,2,1,0:T(8,128)S(1)}, f32[9,5,16,2]{3,2,1,0:T(8,128)S(1)}, u32[]{:S(2)}, u32[]{:S(2)}) collective-permute-start(f32[9,5,16,2]{3,2,1,0:T(8,128)S(1)} %get-tuple-element.29), channel_id=1, source_target_pairs={{1,0},{2,1},{3,2},{4,3},{5,4},{6,5},{7,6},{8,7},{9,8},{10,9},{11,1... | collective-permute-start | bytes 17288 | tf_op jit(solution)/shard_map/ppermute | solution.py:28
  13.7 0.0 collective-permute-start.1
  13.7 0.0 copy-done.2
  13.7 0.7 %fusion.91 = (s32[1,1]{1,0:T(1,128)}, s32[1,1]{1,0:T(1,128)}, s32[1,1]{1,0:T(1,128)}, s32[1,1]{1,0:T(1,128)}, s32[1,1]{1,0:T(1,128)}, /*index=5*/s32[1,1]{1,0:T(1,128)}, s32[1,1]{1,0:T(1,128)}, s32[1,1]{1,0:T(1,128)}) fusion(s32[1,4]{1,0:T(1,128)S(1)} %get-tuple-element.35, s32[1,4]{1,0:T(1,128)S(1)} %get-tuple-element.36), kind=kLoop, calls=%fused_computation.220 | loop fusion | bytes 64 | tf_op jit(solution)/shard_map/slice | solution.py:86
  14.4 0.7 %sine_multiply_fusion = f32[128]{0:T(128)S(1)} fusion(s32[]{:T(128)S(6)} %mul.979, s32[]{:T(128)} %bitcast.9), kind=kLoop, calls=%fused_computation.196 | loop fusion | flops 2048 | bytes 520 | tf_op jit(solution)/shard_map/mul | solution.py:89
  15.1 0.7 %fusion.72 = f32[128]{0:T(128)S(1)} fusion(s32[]{:T(128)S(6)} %mul.979, s32[]{:T(128)} %bitcast.9), kind=kLoop, calls=%fused_computation.201 | loop fusion | flops 1920 | bytes 520 | tf_op jit(solution)/shard_map/cos | solution.py:88
  15.8 0.7 %sine_multiply_fusion.1 = f32[128]{0:T(128)S(1)} fusion(s32[]{:T(128)S(6)} %mul.979, s32[]{:T(128)} %bitcast.8), kind=kLoop, calls=%fused_computation.197 | loop fusion | flops 2048 | bytes 520 | tf_op jit(solution)/shard_map/mul | solution.py:89
  16.6 0.7 %fusion.73 = f32[128]{0:T(128)S(1)} fusion(s32[]{:T(128)S(6)} %mul.979, s32[]{:T(128)} %bitcast.8), kind=kLoop, calls=%fused_computation.202 | loop fusion | flops 1920 | bytes 520 | tf_op jit(solution)/shard_map/cos | solution.py:88
  17.3 0.6 %sine_multiply_fusion.2 = f32[128]{0:T(128)S(1)} fusion(s32[]{:T(128)S(6)} %mul.979, s32[]{:T(128)} %bitcast.7), kind=kLoop, calls=%fused_computation.198 | loop fusion | flops 2048 | bytes 520 | tf_op jit(solution)/shard_map/mul | solution.py:89
  17.9 0.6 %fusion.74 = f32[128]{0:T(128)S(1)} fusion(s32[]{:T(128)S(6)} %mul.979, s32[]{:T(128)} %bitcast.7), kind=kLoop, calls=%fused_computation.203 | loop fusion | flops 1920 | bytes 520 | tf_op jit(solution)/shard_map/cos | solution.py:88
  18.5 0.7 %sine_multiply_fusion.3 = f32[128]{0:T(128)S(1)} fusion(s32[]{:T(128)S(6)} %mul.979, s32[]{:T(128)} %bitcast.6), kind=kLoop, calls=%fused_computation.199 | loop fusion | flops 2048 | bytes 520 | tf_op jit(solution)/shard_map/mul | solution.py:89
  19.2 0.7 %fusion.75 = f32[128]{0:T(128)S(1)} fusion(s32[]{:T(128)S(6)} %mul.979, s32[]{:T(128)} %bitcast.6), kind=kLoop, calls=%fused_computation.204 | loop fusion | flops 1920 | bytes 520 | tf_op jit(solution)/shard_map/cos | solution.py:88
  19.9 0.7 %fusion.82 = f32[128]{0:T(128)S(1)} fusion(s32[]{:T(128)S(6)} %mul.979, s32[]{:T(128)} %bitcast.2), kind=kLoop, calls=%fused_computation.211 | loop fusion | flops 1920 | bytes 520 | tf_op jit(solution)/shard_map/sin | solution.py:89
  20.6 0.7 %fusion.83 = f32[128]{0:T(128)S(1)} fusion(s32[]{:T(128)S(6)} %mul.979, s32[]{:T(128)} %bitcast.2), kind=kLoop, calls=%fused_computation.212 | loop fusion | flops 1920 | bytes 520 | tf_op jit(solution)/shard_map/cos | solution.py:88
  21.3 0.7 %fusion.80 = f32[128]{0:T(128)S(1)} fusion(s32[]{:T(128)S(6)} %mul.979, s32[]{:T(128)} %bitcast.3), kind=kLoop, calls=%fused_computation.209 | loop fusion | flops 1920 | bytes 520 | tf_op jit(solution)/shard_map/sin | solution.py:89
  21.9 0.7 %fusion.81 = f32[128]{0:T(128)S(1)} fusion(s32[]{:T(128)S(6)} %mul.979, s32[]{:T(128)} %bitcast.3), kind=kLoop, calls=%fused_computation.210 | loop fusion | flops 1920 | bytes 520 | tf_op jit(solution)/shard_map/cos | solution.py:88
  22.6 0.7 %fusion.78 = f32[128]{0:T(128)S(1)} fusion(s32[]{:T(128)S(6)} %mul.979, s32[]{:T(128)} %bitcast.4), kind=kLoop, calls=%fused_computation.207 | loop fusion | flops 1920 | bytes 520 | tf_op jit(solution)/shard_map/sin | solution.py:89
  23.3 0.7 %fusion.79 = f32[128]{0:T(128)S(1)} fusion(s32[]{:T(128)S(6)} %mul.979, s32[]{:T(128)} %bitcast.4), kind=kLoop, calls=%fused_computation.208 | loop fusion | flops 1920 | bytes 520 | tf_op jit(solution)/shard_map/cos | solution.py:88
  24.0 0.0 copy-done
  24.0 0.0 copy-start.1
  24.0 0.0 copy-done.3
  24.0 0.6 %fusion.63 = s32[]{:T(128)} fusion(s32[2]{0:T(128)S(1)} %copy-done.3, s32[]{:T(128)S(6)} %axis_index.23), kind=kLoop, calls=%fused_computation.186 | loop fusion | flops 5 | bytes 16 | tf_op jit(solution)/shard_map/reduce_sum | solution.py:108
  25.3 0.7 %fusion.76 = f32[128]{0:T(128)S(1)} fusion(s32[]{:T(128)S(6)} %mul.979, s32[]{:T(128)} %bitcast.5), kind=kLoop, calls=%fused_computation.205 | loop fusion | flops 1920 | bytes 520 | tf_op jit(solution)/shard_map/sin | solution.py:89
  26.1 0.1 multiply_bitcast_fusion.3
  26.2 0.7 %fusion.77 = f32[128]{0:T(128)S(1)} fusion(s32[]{:T(128)S(6)} %mul.979, s32[]{:T(128)} %bitcast.5), kind=kLoop, calls=%fused_computation.206 | loop fusion | flops 1920 | bytes 520 | tf_op jit(solution)/shard_map/cos | solution.py:88
  27.0 0.0 collective-permute-done
  27.2 0.0 copy-done.1
  27.2 0.0 collective-permute-done.3
  27.4 0.2 pad.18
  27.6 0.2 pad.17
  27.7 0.0 collective-permute-done.2
  27.8 0.0 collective-permute-done.1
  27.8 0.5 pad_maximum_fusion
  28.3 0.1 fusion.86
  28.4 0.1 add_reduce_fusion.1
  28.5 0.6 %pad_add_fusion.1 = (f32[9,5,20,132]{3,2,1,0:T(8,128)S(1)}, f32[9,5,20,132]{3,2,1,0:T(8,128)S(1)}) fusion(f32[1,5,20,132]{3,2,1,0:T(8,128)S(1)} %multiply_bitcast_fusion.5, f32[20,132]{1,0:T(8,128)S(1)} %get-tuple-element.15, f32[20,132]{1,0:T(8,128)S(1)} %get-tuple-element.16, f32[9,5,2,132]{3,2,1,0:T(2,128)S(1)} %pad.18, ...), kind=kLoop, calls=%fused_computation.3 | loop fusion | flops 831600 | bytes 1499520 | tf_op jit(solution)/shard_map/add | solution.py:48
  29.1 1.7 %fusion.30 = f32[9,5,16,128]{3,2,1,0:T(8,128)S(1)} fusion(f32[9,5,16,128]{3,2,1,0:T(8,128)S(1)} %bitcast.51, f32[9,5,16,2]{3,2,1,0:T(8,128)S(1)} %collective-permute-done.1, f32[9,5,16,2]{3,2,1,0:T(8,128)S(1)} %collective-permute-done.2, f32[9,5,2,132]{3,2,1,0:T(2,128)S(1)} %pad.17, f32[9,5,2,132]{3,2,1,0:T(2,128)S(1)} %pad.18, ...), kind=kLoop, calls=%fused_computation.58 | loop fusion | flops 3686400 | bytes 2654272 | tf_op jit(solution)/shard_map/add | solution.py:145
  30.9 0.1 multiply_bitcast_fusion.1
  31.0 0.2 fusion.88
  31.2 1.3 %collective-permute-start.7 = (f32[9,5,2,128]{3,2,1,0:T(2,128)S(1)}, f32[9,5,2,128]{3,2,1,0:T(2,128)S(1)}, u32[]{:S(2)}, u32[]{:S(2)}) collective-permute-start(f32[9,5,2,128]{3,2,1,0:T(2,128)S(1)} %get-tuple-element.21), channel_id=1, source_target_pairs={{16,0},{17,1},{18,2},{19,3},{20,4},{21,5},{22,6},{23,7},{24,8},{25... | collective-permute-start | bytes 138248 | tf_op jit(solution)/shard_map/ppermute | solution.py:17
  32.5 3.0 %collective-permute-start.4 = (f32[9,5,2,128]{3,2,1,0:T(2,128)S(1)}, f32[9,5,2,128]{3,2,1,0:T(2,128)S(1)}, u32[]{:S(2)}, u32[]{:S(2)}) collective-permute-start(f32[9,5,2,128]{3,2,1,0:T(2,128)S(1)} %get-tuple-element.22), channel_id=1, source_target_pairs={{0,16},{1,17},{2,18},{3,19},{4,20},{5,21},{6,22},{7,23},{8,24},{9,... | collective-permute-start | bytes 138248 | tf_op jit(solution)/shard_map/ppermute | solution.py:17
  35.6 5.7 %collective-permute-start.6 = (f32[9,5,16,2]{3,2,1,0:T(8,128)S(1)}, f32[9,5,16,2]{3,2,1,0:T(8,128)S(1)}, u32[]{:S(2)}, u32[]{:S(2)}) collective-permute-start(f32[9,5,16,2]{3,2,1,0:T(8,128)S(1)} %get-tuple-element.23), channel_id=1, source_target_pairs={{1,0},{2,1},{3,2},{4,3},{5,4},{6,5},{7,6},{8,7},{9,8},{10,9},{11,1... | collective-permute-start | bytes 17288 | tf_op jit(solution)/shard_map/ppermute | solution.py:28
  41.3 0.0 collective-permute-start.5
  41.3 0.0 collective-permute-done.4
  41.4 0.0 collective-permute-done.7
  41.7 0.2 pad.20
  41.8 0.2 pad.19
  42.0 6.7 %collective-permute-done.6 = f32[9,5,16,2]{3,2,1,0:T(8,128)S(1)} collective-permute-done((f32[9,5,16,2]{3,2,1,0:T(8,128)S(1)}, f32[9,5,16,2]{3,2,1,0:T(8,128)S(1)}, u32[]{:S(2)}, u32[]{:S(2)}) %collective-permute-start.6) | collective-permute-done | bytes 5792 | tf_op jit(solution)/shard_map/ppermute | solution.py:28
  48.7 5.8 %collective-permute-done.5 = f32[9,5,16,2]{3,2,1,0:T(8,128)S(1)} collective-permute-done((f32[9,5,16,2]{3,2,1,0:T(8,128)S(1)}, f32[9,5,16,2]{3,2,1,0:T(8,128)S(1)}, u32[]{:S(2)}, u32[]{:S(2)}) %collective-permute-start.5) | collective-permute-done | bytes 5792 | tf_op jit(solution)/shard_map/ppermute | solution.py:27
  54.5 0.5 pad_maximum_fusion.1
  55.0 0.1 fusion.85
  55.1 0.1 add_reduce_fusion
  55.2 0.6 %pad_add_fusion = (f32[9,5,20,132]{3,2,1,0:T(8,128)S(1)}, f32[9,5,20,132]{3,2,1,0:T(8,128)S(1)}) fusion(f32[1,5,20,132]{3,2,1,0:T(8,128)S(1)} %multiply_bitcast_fusion.4, f32[20,132]{1,0:T(8,128)S(1)} %get-tuple-element.9, f32[20,132]{1,0:T(8,128)S(1)} %get-tuple-element.10, f32[9,5,2,132]{3,2,1,0:T(2,128)S(1)} %pad.20, ...), kind=kLoop, calls=%fused_computation.2 | loop fusion | flops 831600 | bytes 1499520 | tf_op jit(solution)/shard_map/add | solution.py:48
  55.8 2.5 %fusion.16 = f32[1,9,5,16,128]{4,3,2,1,0:T(8,128)} fusion(f32[9,5,16,128]{3,2,1,0:T(8,128)S(1)} %fusion.30, f32[9,5,16,2]{3,2,1,0:T(8,128)S(1)} %collective-permute-done.5, f32[9,5,16,2]{3,2,1,0:T(8,128)S(1)} %collective-permute-done.6, f32[9,5,2,132]{3,2,1,0:T(2,128)S(1)} %pad.19, f32[9,5,2,132]{3,2,1,0:T(2,128)S(1)} %pad.20, ...), kind=kLoop, calls=%fused_computation.33 | loop fusion | flops 3686400 | bytes 3022912 | tf_op jit(solution)/shard_map/broadcast_in_dim | solution.py:146
  (58 shorter events, 0.9 us)
Async XLA Ops:
  0.0 24.0 %copy-start = (f32[1,9,5,16,128]{4,3,2,1,0:T(8,128)S(1)}, f32[1,9,5,16,128]{4,3,2,1,0:T(8,128)}, u32[]{:S(2)}) copy-start(f32[1,9,5,16,128]{4,3,2,1,0:T(8,128)} %param.4) | copy-start | bytes 1105924
  0.0 13.7 %copy-start.2 = (s32[1,4]{1,0:T(1,128)S(1)}, s32[1,4]{1,0:T(1,128)}, u32[]{:S(2)}) copy-start(s32[1,4]{1,0:T(1,128)} %param.7) | copy-start | bytes 52
  0.0 24.0 %copy-start.3 = (s32[2]{0:T(128)S(1)}, s32[2]{0:T(128)}, u32[]{:S(2)}) copy-start(s32[2]{0:T(128)} %param.6) | copy-start | bytes 28
  1.1 26.1 %collective-permute-start.3 = (f32[9,5,2,128]{3,2,1,0:T(2,128)S(1)}, f32[9,5,2,128]{3,2,1,0:T(2,128)S(1)}, u32[]{:S(2)}, u32[]{:S(2)}) collective-permute-start(f32[9,5,2,128]{3,2,1,0:T(2,128)S(1)} %get-tuple-element.27), channel_id=1, source_target_pairs={{16,0},{17,1},{18,2},{19,3},{20,4},{21,5},{22,6},{23,7},{24,8},{25... | collective-permute-start | bytes 138248 | tf_op jit(solution)/shard_map/ppermute | solution.py:17
  2.4 24.6 %collective-permute-start = (f32[9,5,2,128]{3,2,1,0:T(2,128)S(1)}, f32[9,5,2,128]{3,2,1,0:T(2,128)S(1)}, u32[]{:S(2)}, u32[]{:S(2)}) collective-permute-start(f32[9,5,2,128]{3,2,1,0:T(2,128)S(1)} %get-tuple-element.28), channel_id=1, source_target_pairs={{0,16},{1,17},{2,18},{3,19},{4,20},{5,21},{6,22},{7,23},{8,24},{9,... | collective-permute-start | bytes 138248 | tf_op jit(solution)/shard_map/ppermute | solution.py:17
  6.7 21.0 %collective-permute-start.2 = (f32[9,5,16,2]{3,2,1,0:T(8,128)S(1)}, f32[9,5,16,2]{3,2,1,0:T(8,128)S(1)}, u32[]{:S(2)}, u32[]{:S(2)}) collective-permute-start(f32[9,5,16,2]{3,2,1,0:T(8,128)S(1)} %get-tuple-element.29), channel_id=1, source_target_pairs={{1,0},{2,1},{3,2},{4,3},{5,4},{6,5},{7,6},{8,7},{9,8},{10,9},{11,1... | collective-permute-start | bytes 17288 | tf_op jit(solution)/shard_map/ppermute | solution.py:28
  13.7 14.0 %collective-permute-start.1 = (f32[9,5,16,2]{3,2,1,0:T(8,128)S(1)}, f32[9,5,16,2]{3,2,1,0:T(8,128)S(1)}, u32[]{:S(2)}, u32[]{:S(2)}) collective-permute-start(f32[9,5,16,2]{3,2,1,0:T(8,128)S(1)} %get-tuple-element.30), channel_id=1, source_target_pairs={{0,1},{1,2},{2,3},{3,4},{4,5},{5,6},{6,7},{7,8},{8,9},{9,10},{10,1... | collective-permute-start | bytes 17288 | tf_op jit(solution)/shard_map/ppermute | solution.py:27
  24.0 3.2 %copy-start.1 = (f32[9,5,128]{2,1,0:T(8,128)S(1)}, f32[9,5,128]{2,1,0:T(8,128)}, u32[]{:S(2)}) copy-start(f32[9,5,128]{2,1,0:T(8,128)} %param.5) | copy-start | bytes 69124
  31.2 10.3 %collective-permute-start.7 = (f32[9,5,2,128]{3,2,1,0:T(2,128)S(1)}, f32[9,5,2,128]{3,2,1,0:T(2,128)S(1)}, u32[]{:S(2)}, u32[]{:S(2)}) collective-permute-start(f32[9,5,2,128]{3,2,1,0:T(2,128)S(1)} %get-tuple-element.21), channel_id=1, source_target_pairs={{16,0},{17,1},{18,2},{19,3},{20,4},{21,5},{22,6},{23,7},{24,8},{25... | collective-permute-start | bytes 138248 | tf_op jit(solution)/shard_map/ppermute | solution.py:17
  32.5 8.8 %collective-permute-start.4 = (f32[9,5,2,128]{3,2,1,0:T(2,128)S(1)}, f32[9,5,2,128]{3,2,1,0:T(2,128)S(1)}, u32[]{:S(2)}, u32[]{:S(2)}) collective-permute-start(f32[9,5,2,128]{3,2,1,0:T(2,128)S(1)} %get-tuple-element.22), channel_id=1, source_target_pairs={{0,16},{1,17},{2,18},{3,19},{4,20},{5,21},{6,22},{7,23},{8,24},{9,... | collective-permute-start | bytes 138248 | tf_op jit(solution)/shard_map/ppermute | solution.py:17
  35.6 13.1 %collective-permute-start.6 = (f32[9,5,16,2]{3,2,1,0:T(8,128)S(1)}, f32[9,5,16,2]{3,2,1,0:T(8,128)S(1)}, u32[]{:S(2)}, u32[]{:S(2)}) collective-permute-start(f32[9,5,16,2]{3,2,1,0:T(8,128)S(1)} %get-tuple-element.23), channel_id=1, source_target_pairs={{1,0},{2,1},{3,2},{4,3},{5,4},{6,5},{7,6},{8,7},{9,8},{10,9},{11,1... | collective-permute-start | bytes 17288 | tf_op jit(solution)/shard_map/ppermute | solution.py:28
  41.3 13.2 %collective-permute-start.5 = (f32[9,5,16,2]{3,2,1,0:T(8,128)S(1)}, f32[9,5,16,2]{3,2,1,0:T(8,128)S(1)}, u32[]{:S(2)}, u32[]{:S(2)}) collective-permute-start(f32[9,5,16,2]{3,2,1,0:T(8,128)S(1)} %get-tuple-element.24), channel_id=1, source_target_pairs={{0,1},{1,2},{2,3},{3,4},{4,5},{5,6},{6,7},{7,8},{8,9},{9,10},{10,1... | collective-permute-start | bytes 17288 | tf_op jit(solution)/shard_map/ppermute | solution.py:27
where the time goes:
time: 58.7 us; the launch traced here: 58.3 us
  starting transfers between devices  21.3 us (36%)
  other arithmetic  19.1 us (33%)
  waiting for transfers between devices  12.5 us (21%)
  local copies, waits for them, and re-layouts  4.22 us (7%)
  between operations  1.13 us (2%)
    ppermute x2, starting transfers between devices, with_halo(): after = lax.ppermute(leading, axis, down)  12.7 us
    ppermute x4, starting transfers between devices, from_behind(): return lax.ppermute(shard, axis, pairs)  8.64 us
    ppermute x2, waiting for transfers between devices, with_halo(): after = lax.ppermute(leading, axis, down)  6.68 us
    ppermute x2, waiting for transfers between devices, with_halo(): before = lax.ppermute(last, axis, up)  5.8 us
    cos x8, other arithmetic, rotate_modes(): cosine = jnp.cos(angle)  5.51 us
    sin x4, other arithmetic, rotate_modes(): sine = sign * jnp.sin(angle)  2.77 us
    mul x4, other arithmetic, rotate_modes(): sine = sign * jnp.sin(angle)  2.73 us
    broadcast_in_dim x1, other arithmetic, body(): return current[None]  2.45 us
  transfers between devices with their start and end apart: 8, of which 2 were waited for; matrix products, arithmetic and copies ran while one was open for 26% of the time, Pallas kernels for 0%

commit v1 on v0

v1 whole, which is shorter than its diff:
```python
import functools
import math

import jax
import jax.numpy as jnp
from jax import lax
from jax.experimental import pallas as pl
from jax.experimental.pallas import tpu as pltpu
from jax.sharding import PartitionSpec as P

DIFFUSE = 0.05
FOURTH_SMOOTH = 0.03
COURANT = 0.6
FREQ_SCALE = 0.02
MESH = pl.DeviceIdType.MESH
NEAR = DIFFUSE + 4.0 * FOURTH_SMOOTH
CENTER = -4.0 * DIFFUSE - 12.0 * FOURTH_SMOOTH
HALO = 4
PAD = 8


def section(src, base, rows, start, start_base, weight, rates, emit, comps, nvars):
    width = src.shape[2]

    def at(c, v, off):
        return src[c * nvars + v, base + off : base + off + rows, :]

    def opening(v):
        return start[v, start_base : start_base + rows, :]

    coef_up = (NEAR - 0.5) - 0.25 * jnp.tanh(at(0, 1, 1))
    coef_down = (NEAR + 0.5) + 0.25 * jnp.tanh(at(0, 1, -1))
    half_turn = 0.25 * jnp.tanh(at(0, 2, 0))
    coef_next = NEAR - pltpu.roll(half_turn, width - 1, 1)
    coef_prev = NEAR + pltpu.roll(half_turn, 1, 1)
    step = (weight * COURANT) / (
        1.0 + 0.5 * jnp.tanh(opening(1)) + jnp.abs(0.5 * jnp.tanh(opening(2)))
    )

    def one(c, v):
        here, up, down = at(c, v, 0), at(c, v, 1), at(c, v, -1)
        far = (
            at(c, v, 2)
            + at(c, v, -2)
            + pltpu.roll(here, width - 2, 1)
            + pltpu.roll(here, 2, 1)
        )
        total = (
            coef_up * up
            + coef_down * down
            + coef_next * pltpu.roll(here, width - 1, 1)
            + coef_prev * pltpu.roll(here, 1, 1)
            + CENTER * here
            - FOURTH_SMOOTH * far
        )
        return here, up, down, total

    def put(c, v, total):
        k = c * nvars + v
        emit(k, start[k, start_base : start_base + rows, :] + step * total)

    def per_var(v, carry):
        stress = None
        for n in range(1, comps // 2 + 1):
            real, real_up, real_down, real_total = one(2 * n - 1, v)
            imag, imag_up, imag_down, imag_total = one(2 * n, v)
            rate = rates[n - 1]
            put(2 * n - 1, v, real_total + rate * imag)
            put(2 * n, v, imag_total - rate * real)
            term = (
                at(2 * n - 1, 1, 1) * real_up
                + at(2 * n, 1, 1) * imag_up
                - at(2 * n - 1, 1, -1) * real_down
                - at(2 * n, 1, -1) * imag_down
            )
            stress = term if stress is None else stress + term
        _, _, _, total = one(0, v)
        put(0, v, total - 0.25 * stress)
        return carry

    lax.fori_loop(0, nvars, per_var, 0)


def kernel(
    rows_total,
    blocks,
    nvars,
    modes,
    counts,
    state,
    inflow,
    out,
    e_main,
    e_edge,
    f_main,
    f_edge,
    x_main,
    x_edge,
    y_main,
    y_edge,
    in_main,
    in_edge,
    pack,
    halo,
    low,
    high,
    low_halo,
    high_halo,
    local_sem,
    send_sem,
    recv_sem,
):
    fields, depth, width = state.shape
    comps = fields // nvars
    harmonics = comps // 2
    slots = width // HALO
    groups = -(-fields // slots)
    layers = depth // 8
    total_columns = width * blocks
    row = lax.axis_index("row")
    blk = lax.axis_index("blk")
    right = lax.rem(blk + 1, blocks)
    left = lax.rem(blk + blocks - 1, blocks)
    has_low = row > 0
    has_high = row < rows_total - 1

    barrier = pltpu.get_barrier_semaphore()

    def greet(r, b):
        pl.semaphore_signal(barrier, inc=1, device_id={"row": r, "blk": b}, device_id_type=MESH)

    greet(row, right)
    greet(row, left)

    @pl.when(has_high)
    def _():
        greet(row + 1, right)
        greet(row + 1, left)
        greet(row + 1, blk)

    @pl.when(has_low)
    def _():
        greet(row - 1, right)
        greet(row - 1, left)
        greet(row - 1, blk)

    fetch = pltpu.make_async_copy(state, e_main.at[:, PAD : PAD + depth, :], local_sem.at[0])
    fetch_in = pltpu.make_async_copy(inflow, in_main, local_sem.at[1])
    fetch.start()
    fetch_in.start()

    shape = (8, width)
    sub = lax.broadcasted_iota(jnp.int32, shape, 0)
    lane = lax.broadcasted_iota(jnp.int32, shape, 1)
    sign = jnp.where((sub // 2) % 2 == 0, 1.0, -1.0).astype(jnp.float32)

    def mode_of(interface, n):
        value = jnp.int32(0)
        for i in range(rows_total - 1):
            value = value + jnp.where(interface == i, modes[i, n], 0)
        return value

    def count_of(wanted):
        value = jnp.int32(0)
        for i in range(rows_total):
            value = value + jnp.where(wanted == i, counts[i], 0)
        return value.astype(jnp.float32)

    def tables(columns):
        made = []
        for n in range(harmonics):
            mode = jnp.where(sub < 4, mode_of(row - 1, n), mode_of(row, n))
            product = mode * columns
            if total_columns & (total_columns - 1) == 0:
                turns = product & (total_columns - 1)
            else:
                turns = jnp.remainder(product, total_columns)
            angle = (2.0 * math.pi / total_columns) * turns.astype(jnp.float32)
            made.append((jnp.cos(angle), sign * jnp.sin(angle)))
        return made

    tab_main = tables(blk * width + lane)
    tab_edge = tables(blk * width + jnp.where(lane < width // 2, lane - HALO, lane + HALO))
    own_rate = FREQ_SCALE * count_of(row)
    next_rate = jnp.where(sub < 4, FREQ_SCALE * count_of(row - 1), FREQ_SCALE * count_of(row + 1))
    own_rates = [own_rate * float(n) for n in range(1, harmonics + 1)]
    next_rates = [next_rate * float(n) for n in range(1, harmonics + 1)]

    fetch.wait()
    fetch_in.wait()

    def widen(value):
        at_lane = lax.broadcasted_iota(jnp.int32, value.shape, 1)
        return jnp.where(
            at_lane < width // 2,
            pltpu.roll(value, HALO, 1),
            pltpu.roll(value, width - HALO, 1),
        )

    for layer in range(layers):
        for g in range(groups):
            left_edge = jnp.zeros(shape, jnp.float32)
            right_edge = jnp.zeros(shape, jnp.float32)
            for m in range(min(slots, fields - g * slots)):
                start_row = PAD + 8 * layer
                value = e_main[g * slots + m, start_row : start_row + 8, :]
                spot = lane // HALO == m
                left_edge = jnp.where(spot, pltpu.roll(value, HALO * m, 1), left_edge)
                right_edge = jnp.where(
                    spot, pltpu.roll(value, (HALO * m + HALO) % width, 1), right_edge
                )
            pack[0, layer * groups + g] = left_edge
            pack[1, layer * groups + g] = right_edge
    left_edge = jnp.zeros((nvars, width), jnp.float32)
    right_edge = jnp.zeros((nvars, width), jnp.float32)
    lane_in = lax.broadcasted_iota(jnp.int32, (nvars, width), 1)
    for c in range(comps):
        value = in_main[c]
        spot = lane_in // HALO == c
        left_edge = jnp.where(spot, pltpu.roll(value, HALO * c, 1), left_edge)
        right_edge = jnp.where(spot, pltpu.roll(value, (HALO * c + HALO) % width, 1), right_edge)
        in_edge[c] = widen(value)
    pack[0, layers * groups, 0:nvars, :] = left_edge
    pack[1, layers * groups, 0:nvars, :] = right_edge

    greeters = 2 + 3 * has_low.astype(jnp.int32) + 3 * has_high.astype(jnp.int32)
    pl.semaphore_wait(barrier, greeters)

    def send(src, dst, index, r, b):
        return pltpu.make_async_remote_copy(
            src_ref=src,
            dst_ref=dst,
            send_sem=send_sem.at[index],
            recv_sem=recv_sem.at[index],
            device_id={"row": r, "blk": b},
            device_id_type=MESH,
        )

    bottom = pl.ds(0, groups)
    top = pl.ds((layers - 1) * groups, groups)
    level = [send(pack.at[1], halo.at[0], 0, row, right), send(pack.at[0], halo.at[1], 1, row, left)]
    up = [
        send(pack.at[1, top], low_halo.at[0], 2, row + 1, right),
        send(pack.at[0, top], low_halo.at[1], 3, row + 1, left),
        send(state.at[:, pl.ds(depth - 8, 8), :], low, 4, row + 1, blk),
    ]
    down = [
        send(pack.at[1, bottom], high_halo.at[0], 5, row - 1, right),
        send(pack.at[0, bottom], high_halo.at[1], 6, row - 1, left),
        send(state.at[:, pl.ds(0, 8), :], high, 7, row - 1, blk),
    ]
    for copy in level:
        copy.start()

    @pl.when(has_high)
    def _():
        for copy in up:
            copy.start()

    @pl.when(has_low)
    def _():
        for copy in down:
            copy.start()

    for k in range(fields):
        e_edge[k, PAD : PAD + depth, :] = widen(e_main[k, PAD : PAD + depth, :])

    @pl.when(has_low)
    def _():
        up[2].wait_recv()
        x_main[:, 0:4, :] = low[:, 4:8, :]

    @pl.when(jnp.logical_not(has_low))
    def _():
        x_main[:, 0:4, :] = jnp.zeros((fields, 4, width), jnp.float32)

    @pl.when(has_high)
    def _():
        down[2].wait_recv()
        x_main[:, 8:12, :] = high[:, 0:4, :]

    @pl.when(jnp.logical_not(has_high))
    def _():
        x_main[:, 8:12, :] = jnp.zeros((fields, 4, width), jnp.float32)

    def ends(field, inflow_of):
        @pl.when(jnp.logical_not(has_low))
        def _():
            for c in range(comps):
                for v in range(nvars):
                    plane = inflow_of[c, v : v + 1, :]
                    field[c * nvars + v, PAD - 2 : PAD, :] = jnp.broadcast_to(plane, (2, width))

        @pl.when(jnp.logical_not(has_high))
        def _():
            for k in range(fields):
                plane = field[k, PAD + depth - 1 : PAD + depth, :]
                field[k, PAD + depth : PAD + depth + 2, :] = jnp.broadcast_to(plane, (2, width))

    def turn(load, save, table):
        def per_var(v, carry):
            save(v, load(v))
            for n in range(harmonics):
                cosine, sine = table[n]
                real_at, imag_at = (2 * n + 1) * nvars + v, (2 * n + 2) * nvars + v
                real, imag = load(real_at), load(imag_at)
                save(real_at, real * cosine - imag * sine)
                save(imag_at, real * sine + imag * cosine)
            return carry

        lax.fori_loop(0, nvars, per_var, 0)

    def both(e, f, x, y, inflow_of, table, emit):
        x[:, 4:6, :] = e[:, PAD : PAD + 2, :]
        x[:, 6:8, :] = e[:, PAD + depth - 2 : PAD + depth, :]

        def save_first(k, value):
            e[k, PAD - 2 : PAD, :] = value[0:2]
            x[k, 4:8, :] = value[2:6]
            e[k, PAD + depth : PAD + depth + 2, :] = value[6:8]

        turn(lambda k: x[k, 2:10, :], save_first, table)
        ends(e, inflow_of)

        def keep_y(k, value):
            y[k] = value

        def keep_f(k, value):
            f[k, PAD : PAD + depth, :] = value

        section(x, 2, 8, x, 2, 0.5, next_rates, keep_y, comps, nvars)
        section(e, PAD, depth, e, PAD, 0.5, own_rates, keep_f, comps, nvars)

        def save_second(k, value):
            f[k, PAD - 2 : PAD, :] = value[0:2]
            f[k, PAD + depth : PAD + depth + 2, :] = value[6:8]

        turn(lambda k: y[k], save_second, table)
        ends(f, inflow_of)
        section(f, PAD, depth, e, PAD, 1.0, own_rates, emit, comps, nvars)

    def emit_main(k, value):
        out[k] = value

    both(e_main, f_main, x_main, y_main, in_main, tab_main, emit_main)

    for k in range(fields):
        x_edge[k, 0:8, :] = widen(x_main[k, 0:8, :])
        x_edge[k, 8:16, :] = widen(x_main[k, 8:16, :])

    for copy in level:
        copy.wait_recv()

    def mended(value, from_left, from_right, m):
        at_lane = lax.broadcasted_iota(jnp.int32, value.shape, 1)
        left_part = pltpu.roll(from_left, (width - HALO * m) % width, 1)
        right_part = pltpu.roll(from_right, (2 * width - HALO - HALO * m) % width, 1)
        return jnp.where(
            at_lane < HALO, left_part, jnp.where(at_lane >= width - HALO, right_part, value)
        )

    for layer in range(layers):
        for k in range(fields):
            g, m = k // slots, k % slots
            spot = slice(PAD + 8 * layer, PAD + 8 * layer + 8)
            at = layer * groups + g
            e_edge[k, spot, :] = mended(e_edge[k, spot, :], halo[0, at], halo[1, at], m)
    for c in range(comps):
        at = layers * groups
        in_edge[c] = mended(in_edge[c], halo[0, at, 0:nvars, :], halo[1, at, 0:nvars, :], c)

    @pl.when(has_low)
    def _():
        up[0].wait_recv()
        up[1].wait_recv()
        for k in range(fields):
            g, m = k // slots, k % slots
            x_edge[k, 0:4, :] = mended(
                x_edge[k, 0:4, :], low_halo[0, g, 4:8, :], low_halo[1, g, 4:8, :], m
            )

    @pl.when(has_high)
    def _():
        down[0].wait_recv()
        down[1].wait_recv()
        for k in range(fields):
            g, m = k // slots, k % slots
            x_edge[k, 8:12, :] = mended(
                x_edge[k, 8:12, :], high_halo[0, g, 0:4, :], high_halo[1, g, 0:4, :], m
            )

    def emit_edge(k, value):
        at_lane = lax.broadcasted_iota(jnp.int32, value.shape, 1)
        first = at_lane < HALO
        last = at_lane >= width - HALO
        moved = jnp.where(first, pltpu.roll(value, width - HALO, 1), pltpu.roll(value, HALO, 1))
        out[k] = jnp.where(jnp.logical_or(first, last), moved, out[k])

    both(e_edge, f_edge, x_edge, y_edge, in_edge, tab_edge, emit_edge)

    for copy in level:
        copy.wait_send()

    @pl.when(has_high)
    def _():
        for copy in up:
            copy.wait_send()

    @pl.when(has_low)
    def _():
        for copy in down:
            copy.wait_send()


def body(rows_total, blocks, state, inflow, blade_counts, modes):
    _, comps, nvars, depth, width = state.shape
    fields = comps * nvars
    groups = -(-fields // (width // HALO))
    layers = depth // 8
    f32 = jnp.float32

    def buf(*shape):
        return pltpu.VMEM(shape, f32)

    tall = depth + 2 * PAD
    result = pl.pallas_call(
        functools.partial(kernel, rows_total, blocks, nvars),
        out_shape=jax.ShapeDtypeStruct((fields, depth, width), f32),
        in_specs=[
            pl.BlockSpec(memory_space=pltpu.SMEM),
            pl.BlockSpec(memory_space=pltpu.SMEM),
            pl.BlockSpec(memory_space=pl.ANY),
            pl.BlockSpec(memory_space=pl.ANY),
        ],
        out_specs=pl.BlockSpec(memory_space=pltpu.VMEM),
        scratch_shapes=[
            buf(fields, tall, width),
            buf(fields, tall, width),
            buf(fields, tall, width),
            buf(fields, tall, width),
            buf(fields, 16, width),
            buf(fields, 16, width),
            buf(fields, 8, width),
            buf(fields, 8, width),
            buf(comps, nvars, width),
            buf(comps, nvars, width),
            buf(2, layers * groups + 1, 8, width),
            buf(2, layers * groups + 1, 8, width),
            buf(fields, 8, width),
            buf(fields, 8, width),
            buf(2, groups, 8, width),
            buf(2, groups, 8, width),
            pltpu.SemaphoreType.DMA((2,)),
            pltpu.SemaphoreType.DMA((8,)),
            pltpu.SemaphoreType.DMA((8,)),
        ],
        compiler_params=pltpu.CompilerParams(collective_id=0, has_side_effects=True),
    )(modes, blade_counts, state.reshape(fields, depth, width), inflow)
    return result.reshape(1, comps, nvars, depth, width)


def solution(mesh):
    placed = (P("row", None, None, None, "blk"), P(None, None, "blk"), P(), P())
    return jax.shard_map(
        functools.partial(body, mesh.shape["row"], mesh.shape["blk"]),
        mesh=mesh,
        in_specs=placed,
        out_specs=P("row", None, None, None, "blk"),
        check_vma=False,
    )
```

time: 58.7 us -> 17.9 us (0.30)
  starting transfers between devices: 21.3 us -> 0 us
  other arithmetic: 19.1 us -> 0 us
  Pallas kernels: 0 us -> 16 us
  waiting for transfers between devices: 12.5 us -> 0 us
  local copies, waits for them, and re-layouts: 4.22 us -> 1.75 us
  between operations: 1.13 us -> 0.01 us
    ppermute x8 -> x0, starting transfers between devices: 21.3 us -> none  [the longest x2 12.7 us: with_halo(): after = lax.ppermute(leading, axis, down)]
    pallas_call x0 -> x1, Pallas kernels: none -> 16 us  [body(): pl.pallas_call(functools.partial(kernel, rows_total, blocks, nvars), out_...]
    ppermute x8 -> x0, waiting for transfers between devices: 12.5 us -> none  [the longest x2 6.68 us: with_halo(): after = lax.ppermute(leading, axis, down)]
    cos x8 -> x0, other arithmetic: 5.51 us -> none  [rotate_modes(): cosine = jnp.cos(angle)]
    slice x9 -> x0, local copies, waits for them, and re-layouts: 3.46 us -> none  [the longest x2 1.43 us: with_halo(): leading = lax.slice_in_dim(shard, 0, width, axis=dim)]
    add x3 -> x0, other arithmetic: 2.91 us -> none  [the longest x1 1.72 us: body(): current = start_state + weight * step_size * residual(padded, frequency)]
    mul x10 -> x0, other arithmetic: 2.81 us -> none  [the longest x4 2.73 us: rotate_modes(): sine = sign * jnp.sin(angle)]
    sin x4 -> x0, other arithmetic: 2.77 us -> none  [rotate_modes(): sine = sign * jnp.sin(angle)]
  transfers between devices with their start and end apart: 8 -> 0, of which waited for: 2 -> 0; matrix products, arithmetic and copies ran while one was open for 26% -> 0% of each run, Pallas kernels for 0% -> 0%
where the time goes in v1:
time: 17.9 us; the launch traced here: 17.7 us
  Pallas kernels  16 us (89%)
  local copies, waits for them, and re-layouts  1.75 us (10%)
    pallas_call x1, Pallas kernels, body(): pl.pallas_call(functools.partial(kernel, rows_total, blocks, nvars), out_...  16 us
    unnamed x1, local copies, waits for them, and re-layouts  1.75 us

profile of v1, /device:TPU:0, one launch (start us, length us, event | category | flops | bytes accessed | tf_op | source)
XLA Modules:
  0.0 17.7 jit_solution(9526405584422270349)
XLA Ops:
  0.0 16.0 %shard_map.46 = f32[45,16,128]{2,1,0:T(8,128)} custom-call(s32[1,4]{1,0:T(1,128)} %modes.1, s32[2]{0:T(128)} %counts.1, f32[45,16,128]{2,1,0:T(8,128)} %bitcast.3, f32[9,5,128]{2,1,0:T(8,128)} %inflow.1), custom_call_target="tpu_custom_call" | custom-call | tf_op jit(solution)/shard_map/pallas_call | solution.py:426
  16.0 1.7 %copy.6 = f32[1,9,5,16,128]{4,3,2,1,0:T(8,128)} copy(f32[1,9,5,16,128]{4,3,2,1,0:T(8,128)} %bitcast.2) | data formatting | bytes 737280

commit v2 on v1

--- a/solution.py
+++ b/solution.py
@@ -85,8 +85,8 @@
     rows_total,
     blocks,
     nvars,
-    modes,
-    counts,
+    modes_in,
+    counts_in,
     state,
     inflow,
     out,
@@ -101,11 +101,14 @@
     in_main,
     in_edge,
     pack,
+    corner,
     halo,
     low,
     high,
     low_halo,
     high_halo,
+    modes,
+    counts,
     local_sem,
     send_sem,
     recv_sem,
@@ -114,7 +117,7 @@
     comps = fields // nvars
     harmonics = comps // 2
     slots = width // HALO
-    groups = -(-fields // slots)
+    groups = -(-(fields + comps) // slots)
     layers = depth // 8
     total_columns = width * blocks
     row = lax.axis_index("row")
@@ -146,8 +149,12 @@
 
     fetch = pltpu.make_async_copy(state, e_main.at[:, PAD : PAD + depth, :], local_sem.at[0])
     fetch_in = pltpu.make_async_copy(inflow, in_main, local_sem.at[1])
-    fetch.start()
-    fetch_in.start()
+    fetch_modes = pltpu.make_async_copy(modes_in, modes, local_sem.at[2])
+    fetch_counts = pltpu.make_async_copy(counts_in, counts, local_sem.at[3])
+    for copy in (fetch_modes, fetch_counts, fetch, fetch_in):
+        copy.start()
+    fetch_modes.wait()
+    fetch_counts.wait()
 
     shape = (8, width)
     sub = lax.broadcasted_iota(jnp.int32, shape, 0)
@@ -201,7 +208,7 @@
         for g in range(groups):
             left_edge = jnp.zeros(shape, jnp.float32)
             right_edge = jnp.zeros(shape, jnp.float32)
-            for m in range(min(slots, fields - g * slots)):
+            for m in range(max(0, min(slots, fields - g * slots))):
                 start_row = PAD + 8 * layer
                 value = e_main[g * slots + m, start_row : start_row + 8, :]
                 spot = lane // HALO == m
@@ -211,17 +218,27 @@
                 )
             pack[0, layer * groups + g] = left_edge
             pack[1, layer * groups + g] = right_edge
-    left_edge = jnp.zeros((nvars, width), jnp.float32)
-    right_edge = jnp.zeros((nvars, width), jnp.float32)
     lane_in = lax.broadcasted_iota(jnp.int32, (nvars, width), 1)
+    for g in range(fields // slots, groups):
+        left_edge = pack[0, g, 0:nvars, :]
+        right_edge = pack[1, g, 0:nvars, :]
+        for c in range(comps):
+            m = fields + c - g * slots
+            if 0 <= m < slots:
+                value = in_main[c]
+                spot = lane_in // HALO == m
+                left_edge = jnp.where(spot, pltpu.roll(value, HALO * m, 1), left_edge)
+                right_edge = jnp.where(
+                    spot, pltpu.roll(value, (HALO * m + HALO) % width, 1), right_edge
+                )
+        pack[0, g, 0:nvars, :] = left_edge
+        pack[1, g, 0:nvars, :] = right_edge
     for c in range(comps):
-        value = in_main[c]
-        spot = lane_in // HALO == c
-        left_edge = jnp.where(spot, pltpu.roll(value, HALO * c, 1), left_edge)
-        right_edge = jnp.where(spot, pltpu.roll(value, (HALO * c + HALO) % width, 1), right_edge)
-        in_edge[c] = widen(value)
-    pack[0, layers * groups, 0:nvars, :] = left_edge
-    pack[1, layers * groups, 0:nvars, :] = right_edge
+        in_edge[c] = widen(in_main[c])
+    for side in range(2):
+        for g in range(groups):
+            corner[0, side, 2 * g : 2 * g + 2, :] = pack[side, g, 0:2, :]
+            corner[1, side, 2 * g : 2 * g + 2, :] = pack[side, (layers - 1) * groups + g, 6:8, :]
 
     greeters = 2 + 3 * has_low.astype(jnp.int32) + 3 * has_high.astype(jnp.int32)
     pl.semaphore_wait(barrier, greeters)
@@ -236,17 +253,15 @@
             device_id_type=MESH,
         )
 
-    bottom = pl.ds(0, groups)
-    top = pl.ds((layers - 1) * groups, groups)
     level = [send(pack.at[1], halo.at[0], 0, row, right), send(pack.at[0], halo.at[1], 1, row, left)]
     up = [
-        send(pack.at[1, top], low_halo.at[0], 2, row + 1, right),
-        send(pack.at[0, top], low_halo.at[1], 3, row + 1, left),
+        send(corner.at[1, 1], low_halo.at[0], 2, row + 1, right),
+        send(corner.at[1, 0], low_halo.at[1], 3, row + 1, left),
         send(state.at[:, pl.ds(depth - 8, 8), :], low, 4, row + 1, blk),
     ]
     down = [
-        send(pack.at[1, bottom], high_halo.at[0], 5, row - 1, right),
-        send(pack.at[0, bottom], high_halo.at[1], 6, row - 1, left),
+        send(corner.at[0, 1], high_halo.at[0], 5, row - 1, right),
+        send(corner.at[0, 0], high_halo.at[1], 6, row - 1, left),
         send(state.at[:, pl.ds(0, 8), :], high, 7, row - 1, blk),
     ]
     for copy in level:
@@ -366,8 +381,8 @@
             at = layer * groups + g
             e_edge[k, spot, :] = mended(e_edge[k, spot, :], halo[0, at], halo[1, at], m)
     for c in range(comps):
-        at = layers * groups
-        in_edge[c] = mended(in_edge[c], halo[0, at, 0:nvars, :], halo[1, at, 0:nvars, :], c)
+        g, m = (fields + c) // slots, (fields + c) % slots
+        in_edge[c] = mended(in_edge[c], halo[0, g, 0:nvars, :], halo[1, g, 0:nvars, :], m)
 
     @pl.when(has_low)
     def _():
@@ -375,8 +390,9 @@
         up[1].wait_recv()
         for k in range(fields):
             g, m = k // slots, k % slots
-            x_edge[k, 0:4, :] = mended(
-                x_edge[k, 0:4, :], low_halo[0, g, 4:8, :], low_halo[1, g, 4:8, :], m
+            spot = slice(2 * g, 2 * g + 2)
+            x_edge[k, 2:4, :] = mended(
+                x_edge[k, 2:4, :], low_halo[0, spot, :], low_halo[1, spot, :], m
             )
 
     @pl.when(has_high)
@@ -385,8 +401,9 @@
         down[1].wait_recv()
         for k in range(fields):
             g, m = k // slots, k % slots
-            x_edge[k, 8:12, :] = mended(
-                x_edge[k, 8:12, :], high_halo[0, g, 0:4, :], high_halo[1, g, 0:4, :], m
+            spot = slice(2 * g, 2 * g + 2)
+            x_edge[k, 8:10, :] = mended(
+                x_edge[k, 8:10, :], high_halo[0, spot, :], high_halo[1, spot, :], m
             )
 
     def emit_edge(k, value):
@@ -415,7 +432,8 @@
 def body(rows_total, blocks, state, inflow, blade_counts, modes):
     _, comps, nvars, depth, width = state.shape
     fields = comps * nvars
-    groups = -(-fields // (width // HALO))
+    groups = -(-(fields + comps) // (width // HALO))
+    corner_rows = -(-2 * groups // 8) * 8
     layers = depth // 8
     f32 = jnp.float32
 
@@ -427,10 +445,10 @@
         functools.partial(kernel, rows_total, blocks, nvars),
         out_shape=jax.ShapeDtypeStruct((fields, depth, width), f32),
         in_specs=[
-            pl.BlockSpec(memory_space=pltpu.SMEM),
-            pl.BlockSpec(memory_space=pltpu.SMEM),
-            pl.BlockSpec(memory_space=pl.ANY),
-            pl.BlockSpec(memory_space=pl.ANY),
+            pl.BlockSpec(memory_space=pltpu.HBM),
+            pl.BlockSpec(memory_space=pltpu.HBM),
+            pl.BlockSpec(memory_space=pltpu.HBM),
+            pl.BlockSpec(memory_space=pltpu.HBM),
         ],
         out_specs=pl.BlockSpec(memory_space=pltpu.VMEM),
         scratch_shapes=[
@@ -444,18 +462,28 @@
             buf(fields, 8, width),
             buf(comps, nvars, width),
             buf(comps, nvars, width),
-            buf(2, layers * groups + 1, 8, width),
-            buf(2, layers * groups + 1, 8, width),
+            buf(2, layers * groups, 8, width),
+            buf(2, 2, corner_rows, width),
+            buf(2, layers * groups, 8, width),
             buf(fields, 8, width),
             buf(fields, 8, width),
-            buf(2, groups, 8, width),
-            buf(2, groups, 8, width),
-            pltpu.SemaphoreType.DMA((2,)),
+            buf(2, corner_rows, width),
+            buf(2, corner_rows, width),
+            pltpu.SMEM(modes.shape, jnp.int32),
+            pltpu.SMEM(blade_counts.shape, jnp.int32),
+            pltpu.SemaphoreType.DMA((4,)),
             pltpu.SemaphoreType.DMA((8,)),
             pltpu.SemaphoreType.DMA((8,)),
         ],
-        compiler_params=pltpu.CompilerParams(collective_id=0, has_side_effects=True),
-    )(modes, blade_counts, state.reshape(fields, depth, width), inflow)
+        compiler_params=pltpu.CompilerParams(
+            collective_id=0, has_side_effects=True, vmem_limit_bytes=16 << 20
+        ),
+    )(
+        *(
+            pltpu.with_memory_space_constraint(value, pltpu.HBM)
+            for value in (modes, blade_counts, state.reshape(fields, depth, width), inflow)
+        )
+    )
     return result.reshape(1, comps, nvars, depth, width)
 
 

time: 17.9 us -> 15.5 us (0.87)
  Pallas kernels: 16 us -> 14.6 us
  local copies, waits for them, and re-layouts: 1.75 us -> 0.74 us
    pallas_call x1, Pallas kernels: 16 us -> 14.6 us  [body(): pl.pallas_call(functools.partial(kernel, rows_total, blocks, nvars), out_...]
    unnamed x1, local copies, waits for them, and re-layouts: 1.75 us -> 0.74 us
where the time goes in v2:
time: 15.5 us; the launch traced here: 15.3 us
  Pallas kernels  14.6 us (94%)
  local copies, waits for them, and re-layouts  0.74 us (5%)
    pallas_call x1, Pallas kernels, body(): pl.pallas_call(functools.partial(kernel, rows_total, blocks, nvars), out_...  14.6 us
    unnamed x1, local copies, waits for them, and re-layouts  0.74 us

profile of v2, /device:TPU:0, one launch (start us, length us, event | category | flops | bytes accessed | tf_op | source)
XLA Modules:
  0.0 15.3 jit_solution(13901820657798577021)
XLA Ops:
  0.0 14.6 %shard_map.46 = f32[45,16,128]{2,1,0:T(8,128)S(1)} custom-call(s32[1,4]{1,0:T(1,128)} %modes_in.1, s32[2]{0:T(128)} %counts_in.1, f32[45,16,128]{2,1,0:T(8,128)} %bitcast.3, f32[9,5,128]{2,1,0:T(8,128)} %inflow.1), custom_call_target="tpu_custom_call" | custom-call | tf_op jit(solution)/shard_map/pallas_call | solution.py:444
  14.6 0.7 %copy.6 = f32[1,9,5,16,128]{4,3,2,1,0:T(8,128)} copy(f32[1,9,5,16,128]{4,3,2,1,0:T(8,128)S(1)} %bitcast.2) | data formatting | bytes 737280

commit v3 on v2

--- a/solution.py
+++ b/solution.py
@@ -17,6 +17,12 @@
 CENTER = -4.0 * DIFFUSE - 12.0 * FOURTH_SMOOTH
 HALO = 4
 PAD = 8
+
+
+def packing(items, layers, width):
+    seg = width // (layers + 2)
+    slots = width // (layers * seg) * (seg // HALO)
+    return seg, -(-items // slots)
 
 
 def section(src, base, rows, start, start_base, weight, rates, emit, comps, nvars):
@@ -95,9 +101,7 @@
     f_main,
     f_edge,
     x_main,
-    x_edge,
     y_main,
-    y_edge,
     in_main,
     in_edge,
     pack,
@@ -116,9 +120,10 @@
     fields, depth, width = state.shape
     comps = fields // nvars
     harmonics = comps // 2
-    slots = width // HALO
-    groups = -(-(fields + comps) // slots)
     layers = depth // 8
+    seg, groups = packing(fields + comps, layers, width)
+    per = seg // HALO
+    slots = width // (layers * seg) * per
     total_columns = width * blocks
     row = lax.axis_index("row")
     blk = lax.axis_index("blk")
@@ -173,72 +178,78 @@
             value = value + jnp.where(wanted == i, counts[i], 0)
         return value.astype(jnp.float32)
 
-    def tables(columns):
+    def tables(modes_at, columns):
         made = []
         for n in range(harmonics):
-            mode = jnp.where(sub < 4, mode_of(row - 1, n), mode_of(row, n))
-            product = mode * columns
+            product = modes_at(n) * columns
             if total_columns & (total_columns - 1) == 0:
                 turns = product & (total_columns - 1)
             else:
                 turns = jnp.remainder(product, total_columns)
             angle = (2.0 * math.pi / total_columns) * turns.astype(jnp.float32)
-            made.append((jnp.cos(angle), sign * jnp.sin(angle)))
+            made.append((jnp.cos(angle), jnp.sin(angle)))
         return made
 
-    tab_main = tables(blk * width + lane)
-    tab_edge = tables(blk * width + jnp.where(lane < width // 2, lane - HALO, lane + HALO))
+    tab_main = [
+        (cosine, sign * sine)
+        for cosine, sine in tables(
+            lambda n: jnp.where(sub < 4, mode_of(row - 1, n), mode_of(row, n)), blk * width + lane
+        )
+    ]
+    part, off = lane // seg, lane % seg
+    edge_column = jnp.where(off < 3 * HALO, off - HALO, off + width - 5 * HALO)
+
+    def edge_mode(n):
+        lower, upper = mode_of(row - 1, n), mode_of(row, n)
+        rising = jnp.where(part == 0, lower, jnp.where(part == layers, upper, 0))
+        falling = jnp.where(part == 1, -lower, jnp.where(part == layers + 1, -upper, 0))
+        return jnp.where(sub < 4, falling, rising)
+
+    tab_edge = tables(edge_mode, blk * width + edge_column)
     own_rate = FREQ_SCALE * count_of(row)
     next_rate = jnp.where(sub < 4, FREQ_SCALE * count_of(row - 1), FREQ_SCALE * count_of(row + 1))
     own_rates = [own_rate * float(n) for n in range(1, harmonics + 1)]
+    edge_rate = jnp.where(
+        part == 0,
+        FREQ_SCALE * count_of(row - 1),
+        jnp.where(part == layers + 1, FREQ_SCALE * count_of(row + 1), own_rate),
+    )
+    edge_rates = [edge_rate * float(n) for n in range(1, harmonics + 1)]
     next_rates = [next_rate * float(n) for n in range(1, harmonics + 1)]
 
     fetch.wait()
     fetch_in.wait()
 
-    def widen(value):
-        at_lane = lax.broadcasted_iota(jnp.int32, value.shape, 1)
-        return jnp.where(
-            at_lane < width // 2,
-            pltpu.roll(value, HALO, 1),
-            pltpu.roll(value, width - HALO, 1),
-        )
-
-    for layer in range(layers):
-        for g in range(groups):
-            left_edge = jnp.zeros(shape, jnp.float32)
-            right_edge = jnp.zeros(shape, jnp.float32)
-            for m in range(max(0, min(slots, fields - g * slots))):
-                start_row = PAD + 8 * layer
-                value = e_main[g * slots + m, start_row : start_row + 8, :]
-                spot = lane // HALO == m
-                left_edge = jnp.where(spot, pltpu.roll(value, HALO * m, 1), left_edge)
-                right_edge = jnp.where(
-                    spot, pltpu.roll(value, (HALO * m + HALO) % width, 1), right_edge
-                )
-            pack[0, layer * groups + g] = left_edge
-            pack[1, layer * groups + g] = right_edge
+    def shifted(value, by):
+        return pltpu.roll(value, by % width, 1)
+
+    def spot_of(item):
+        g, m = item // slots, item % slots
+        return g, (m % per) * HALO + (m // per) * layers * seg
+
+    for g in range(groups):
+        edges = [jnp.zeros(shape, jnp.float32), jnp.zeros(shape, jnp.float32)]
+        for k in range(g * slots, min((g + 1) * slots, fields)):
+            _, p = spot_of(k)
+            for layer in range(layers):
+                q = p + layer * seg
+                value = e_main[k, PAD + 8 * layer : PAD + 8 * layer + 8, :]
+                spot = lane // HALO == q // HALO
+                edges[0] = jnp.where(spot, shifted(value, q), edges[0])
+                edges[1] = jnp.where(spot, shifted(value, q + HALO), edges[1])
+        pack[0, g] = edges[0]
+        pack[1, g] = edges[1]
     lane_in = lax.broadcasted_iota(jnp.int32, (nvars, width), 1)
-    for g in range(fields // slots, groups):
-        left_edge = pack[0, g, 0:nvars, :]
-        right_edge = pack[1, g, 0:nvars, :]
-        for c in range(comps):
-            m = fields + c - g * slots
-            if 0 <= m < slots:
-                value = in_main[c]
-                spot = lane_in // HALO == m
-                left_edge = jnp.where(spot, pltpu.roll(value, HALO * m, 1), left_edge)
-                right_edge = jnp.where(
-                    spot, pltpu.roll(value, (HALO * m + HALO) % width, 1), right_edge
-                )
-        pack[0, g, 0:nvars, :] = left_edge
-        pack[1, g, 0:nvars, :] = right_edge
     for c in range(comps):
-        in_edge[c] = widen(in_main[c])
+        g, p = spot_of(fields + c)
+        spot = lane_in // HALO == p // HALO
+        value = in_main[c]
+        pack[0, g, 0:nvars, :] = jnp.where(spot, shifted(value, p), pack[0, g, 0:nvars, :])
+        pack[1, g, 0:nvars, :] = jnp.where(spot, shifted(value, p + HALO), pack[1, g, 0:nvars, :])
     for side in range(2):
         for g in range(groups):
             corner[0, side, 2 * g : 2 * g + 2, :] = pack[side, g, 0:2, :]
-            corner[1, side, 2 * g : 2 * g + 2, :] = pack[side, (layers - 1) * groups + g, 6:8, :]
+            corner[1, side, 2 * g : 2 * g + 2, :] = pack[side, g, 6:8, :]
 
     greeters = 2 + 3 * has_low.astype(jnp.int32) + 3 * has_high.astype(jnp.int32)
     pl.semaphore_wait(barrier, greeters)
@@ -277,13 +288,30 @@
         for copy in down:
             copy.start()
 
+    def place(value, where_to):
+        at_off = lax.broadcasted_iota(jnp.int32, value.shape, 1) % seg
+        start = where_to * seg
+        return jnp.where(
+            at_off < 3 * HALO,
+            shifted(value, start + HALO),
+            shifted(value, start + 5 * HALO - width),
+        )
+
     for k in range(fields):
-        e_edge[k, PAD : PAD + depth, :] = widen(e_main[k, PAD : PAD + depth, :])
+        value = jnp.zeros(shape, jnp.float32)
+        for layer in range(layers):
+            plane = e_main[k, PAD + 8 * layer : PAD + 8 * layer + 8, :]
+            value = jnp.where(part == layer + 1, place(plane, layer + 1), value)
+        e_edge[k, 2:10, :] = value
+    for c in range(comps):
+        in_edge[c] = place(in_main[c], 1)
 
     @pl.when(has_low)
     def _():
         up[2].wait_recv()
         x_main[:, 0:4, :] = low[:, 4:8, :]
+        for k in range(fields):
+            e_edge[k, 2:10, :] = jnp.where(part == 0, place(low[k], 0), e_edge[k, 2:10, :])
 
     @pl.when(jnp.logical_not(has_low))
     def _():
@@ -293,6 +321,10 @@
     def _():
         down[2].wait_recv()
         x_main[:, 8:12, :] = high[:, 0:4, :]
+        for k in range(fields):
+            e_edge[k, 2:10, :] = jnp.where(
+                part == layers + 1, place(high[k], layers + 1), e_edge[k, 2:10, :]
+            )
 
     @pl.when(jnp.logical_not(has_high))
     def _():
@@ -359,40 +391,48 @@
 
     both(e_main, f_main, x_main, y_main, in_main, tab_main, emit_main)
 
-    for k in range(fields):
-        x_edge[k, 0:8, :] = widen(x_main[k, 0:8, :])
-        x_edge[k, 8:16, :] = widen(x_main[k, 8:16, :])
-
     for copy in level:
         copy.wait_recv()
 
-    def mended(value, from_left, from_right, m):
+    def beyond(value, from_left, from_right, p, start, first, last):
         at_lane = lax.broadcasted_iota(jnp.int32, value.shape, 1)
-        left_part = pltpu.roll(from_left, (width - HALO * m) % width, 1)
-        right_part = pltpu.roll(from_right, (2 * width - HALO - HALO * m) % width, 1)
-        return jnp.where(
-            at_lane < HALO, left_part, jnp.where(at_lane >= width - HALO, right_part, value)
-        )
-
-    for layer in range(layers):
-        for k in range(fields):
-            g, m = k // slots, k % slots
-            spot = slice(PAD + 8 * layer, PAD + 8 * layer + 8)
-            at = layer * groups + g
-            e_edge[k, spot, :] = mended(e_edge[k, spot, :], halo[0, at], halo[1, at], m)
-    for c in range(comps):
-        g, m = (fields + c) // slots, (fields + c) % slots
-        in_edge[c] = mended(in_edge[c], halo[0, g, 0:nvars, :], halo[1, g, 0:nvars, :], m)
+        at_part, at_off = at_lane // seg, at_lane % seg
+        here = jnp.logical_and(at_part >= first, at_part <= last)
+        in_left = jnp.logical_and(here, at_off < HALO)
+        in_right = jnp.logical_and(here, at_off >= 5 * HALO)
+        left_part = shifted(from_left, start - p)
+        right_part = shifted(from_right, start + 5 * HALO - p)
+        return jnp.where(in_left, left_part, jnp.where(in_right, right_part, value))
+
+    for k in range(fields):
+        g, p = spot_of(k)
+        e_edge[k, 2:10, :] = beyond(
+            e_edge[k, 2:10, :], halo[0, g], halo[1, g], p, seg, 1, layers
+        )
 
     @pl.when(has_low)
     def _():
         up[0].wait_recv()
         up[1].wait_recv()
         for k in range(fields):
-            g, m = k // slots, k % slots
+            g, p = spot_of(k)
             spot = slice(2 * g, 2 * g + 2)
-            x_edge[k, 2:4, :] = mended(
-                x_edge[k, 2:4, :], low_halo[0, spot, :], low_halo[1, spot, :], m
+            e_edge[k, 8:10, :] = beyond(
+                e_edge[k, 8:10, :],
+                low_halo[0, spot, :],
+                low_halo[1, spot, :],
+                p + (layers - 1) * seg,
+                0,
+                0,
+                0,
+            )
+
+    @pl.when(jnp.logical_not(has_low))
+    def _():
+        for c in range(comps):
+            g, p = spot_of(fields + c)
+            in_edge[c] = beyond(
+                in_edge[c], halo[0, g, 0:nvars, :], halo[1, g, 0:nvars, :], p, seg, 1, 1
             )
 
     @pl.when(has_high)
@@ -400,20 +440,59 @@
         down[0].wait_recv()
         down[1].wait_recv()
         for k in range(fields):
-            g, m = k // slots, k % slots
+            g, p = spot_of(k)
             spot = slice(2 * g, 2 * g + 2)
-            x_edge[k, 8:10, :] = mended(
-                x_edge[k, 8:10, :], high_halo[0, spot, :], high_halo[1, spot, :], m
+            e_edge[k, 2:4, :] = beyond(
+                e_edge[k, 2:4, :],
+                high_halo[0, spot, :],
+                high_halo[1, spot, :],
+                p,
+                (layers + 1) * seg,
+                layers + 1,
+                layers + 1,
             )
 
+    def link(field):
+        def save(k, value):
+            field[k, 0:2, :] = shifted(value, seg)[6:8]
+            field[k, 10:12, :] = shifted(value, -seg)[0:2]
+
+        turn(lambda k: field[k, 2:10, :], save, tab_edge)
+        two = lax.broadcasted_iota(jnp.int32, (2, width), 1) // seg
+
+        @pl.when(jnp.logical_not(has_low))
+        def _():
+            for c in range(comps):
+                for v in range(nvars):
+                    k = c * nvars + v
+                    plane = jnp.broadcast_to(in_edge[c, v : v + 1, :], (2, width))
+                    field[k, 0:2, :] = jnp.where(two == 1, plane, field[k, 0:2, :])
+
+        @pl.when(jnp.logical_not(has_high))
+        def _():
+            for k in range(fields):
+                plane = jnp.broadcast_to(field[k, 9:10, :], (2, width))
+                field[k, 10:12, :] = jnp.where(two == layers, plane, field[k, 10:12, :])
+
+    def keep_edge(k, value):
+        f_edge[k, 2:10, :] = value
+
     def emit_edge(k, value):
-        at_lane = lax.broadcasted_iota(jnp.int32, value.shape, 1)
-        first = at_lane < HALO
-        last = at_lane >= width - HALO
-        moved = jnp.where(first, pltpu.roll(value, width - HALO, 1), pltpu.roll(value, HALO, 1))
-        out[k] = jnp.where(jnp.logical_or(first, last), moved, out[k])
-
-    both(e_edge, f_edge, x_edge, y_edge, in_edge, tab_edge, emit_edge)
+        first = lane < HALO
+        last = lane >= width - HALO
+        outer = jnp.logical_or(first, last)
+        for layer in range(layers):
+            start = (layer + 1) * seg + HALO
+            moved = jnp.where(
+                first, shifted(value, -start), shifted(value, width - 4 * HALO - start)
+            )
+            rows = slice(8 * layer, 8 * layer + 8)
+            out[k, rows, :] = jnp.where(outer, moved, out[k, rows, :])
+
+    link(e_edge)
+    section(e_edge, 2, 8, e_edge, 2, 0.5, edge_rates, keep_edge, comps, nvars)
+    link(f_edge)
+    section(f_edge, 2, 8, e_edge, 2, 1.0, edge_rates, emit_edge, comps, nvars)
 
     for copy in level:
         copy.wait_send()
@@ -432,9 +511,8 @@
 def body(rows_total, blocks, state, inflow, blade_counts, modes):
     _, comps, nvars, depth, width = state.shape
     fields = comps * nvars
-    groups = -(-(fields + comps) // (width // HALO))
+    _, groups = packing(fields + comps, depth // 8, width)
     corner_rows = -(-2 * groups // 8) * 8
-    layers = depth // 8
     f32 = jnp.float32
 
     def buf(*shape):
@@ -453,18 +531,16 @@
         out_specs=pl.BlockSpec(memory_space=pltpu.VMEM),
         scratch_shapes=[
             buf(fields, tall, width),
-            buf(fields, tall, width),
-            buf(fields, tall, width),
+            buf(fields, 16, width),
             buf(fields, tall, width),
             buf(fields, 16, width),
             buf(fields, 16, width),
             buf(fields, 8, width),
-            buf(fields, 8, width),
             buf(comps, nvars, width),
             buf(comps, nvars, width),
-            buf(2, layers * groups, 8, width),
+            buf(2, groups, 8, width),
             buf(2, 2, corner_rows, width),
-            buf(2, layers * groups, 8, width),
+            buf(2, groups, 8, width),
             buf(fields, 8, width),
             buf(fields, 8, width),
             buf(2, corner_rows, width),

time: 15.5 us -> 15.2 us (0.981)
  Pallas kernels: 14.6 us -> 14.3 us
    pallas_call x1, Pallas kernels: 14.6 us -> 14.3 us  [body(): pl.pallas_call(functools.partial(kernel, rows_total, blocks, nvars), out_...]
where the time goes in v3:
time: 15.2 us; the launch traced here: 15 us
  Pallas kernels  14.3 us (94%)
  local copies, waits for them, and re-layouts  0.74 us (5%)
    pallas_call x1, Pallas kernels, body(): pl.pallas_call(functools.partial(kernel, rows_total, blocks, nvars), out_...  14.3 us
    unnamed x1, local copies, waits for them, and re-layouts  0.74 us

profile of v3, /device:TPU:0, one launch (start us, length us, event | category | flops | bytes accessed | tf_op | source)
XLA Modules:
  0.0 15.0 jit_solution(3275538859240679646)
XLA Ops:
  0.0 14.3 %shard_map.46 = f32[45,16,128]{2,1,0:T(8,128)S(1)} custom-call(s32[1,4]{1,0:T(1,128)} %modes_in.1, s32[2]{0:T(128)} %counts_in.1, f32[45,16,128]{2,1,0:T(8,128)} %bitcast.3, f32[9,5,128]{2,1,0:T(8,128)} %inflow.1), custom_call_target="tpu_custom_call" | custom-call | tf_op jit(solution)/shard_map/pallas_call | solution.py:522
  14.3 0.7 %copy.6 = f32[1,9,5,16,128]{4,3,2,1,0:T(8,128)} copy(f32[1,9,5,16,128]{4,3,2,1,0:T(8,128)S(1)} %bitcast.2) | data formatting | bytes 737280

commit v4 on v3

--- a/solution.py
+++ b/solution.py
@@ -84,7 +84,7 @@
         put(0, v, total - 0.25 * stress)
         return carry
 
-    lax.fori_loop(0, nvars, per_var, 0)
+    lax.fori_loop(0, nvars, per_var, 0, unroll=True)
 
 
 def kernel(
@@ -156,67 +156,13 @@
     fetch_in = pltpu.make_async_copy(inflow, in_main, local_sem.at[1])
     fetch_modes = pltpu.make_async_copy(modes_in, modes, local_sem.at[2])
     fetch_counts = pltpu.make_async_copy(counts_in, counts, local_sem.at[3])
-    for copy in (fetch_modes, fetch_counts, fetch, fetch_in):
+    for copy in (fetch, fetch_in, fetch_modes, fetch_counts):
         copy.start()
-    fetch_modes.wait()
-    fetch_counts.wait()
 
     shape = (8, width)
     sub = lax.broadcasted_iota(jnp.int32, shape, 0)
     lane = lax.broadcasted_iota(jnp.int32, shape, 1)
-    sign = jnp.where((sub // 2) % 2 == 0, 1.0, -1.0).astype(jnp.float32)
-
-    def mode_of(interface, n):
-        value = jnp.int32(0)
-        for i in range(rows_total - 1):
-            value = value + jnp.where(interface == i, modes[i, n], 0)
-        return value
-
-    def count_of(wanted):
-        value = jnp.int32(0)
-        for i in range(rows_total):
-            value = value + jnp.where(wanted == i, counts[i], 0)
-        return value.astype(jnp.float32)
-
-    def tables(modes_at, columns):
-        made = []
-        for n in range(harmonics):
-            product = modes_at(n) * columns
-            if total_columns & (total_columns - 1) == 0:
-                turns = product & (total_columns - 1)
-            else:
-                turns = jnp.remainder(product, total_columns)
-            angle = (2.0 * math.pi / total_columns) * turns.astype(jnp.float32)
-            made.append((jnp.cos(angle), jnp.sin(angle)))
-        return made
-
-    tab_main = [
-        (cosine, sign * sine)
-        for cosine, sine in tables(
-            lambda n: jnp.where(sub < 4, mode_of(row - 1, n), mode_of(row, n)), blk * width + lane
-        )
-    ]
     part, off = lane // seg, lane % seg
-    edge_column = jnp.where(off < 3 * HALO, off - HALO, off + width - 5 * HALO)
-
-    def edge_mode(n):
-        lower, upper = mode_of(row - 1, n), mode_of(row, n)
-        rising = jnp.where(part == 0, lower, jnp.where(part == layers, upper, 0))
-        falling = jnp.where(part == 1, -lower, jnp.where(part == layers + 1, -upper, 0))
-        return jnp.where(sub < 4, falling, rising)
-
-    tab_edge = tables(edge_mode, blk * width + edge_column)
-    own_rate = FREQ_SCALE * count_of(row)
-    next_rate = jnp.where(sub < 4, FREQ_SCALE * count_of(row - 1), FREQ_SCALE * count_of(row + 1))
-    own_rates = [own_rate * float(n) for n in range(1, harmonics + 1)]
-    edge_rate = jnp.where(
-        part == 0,
-        FREQ_SCALE * count_of(row - 1),
-        jnp.where(part == layers + 1, FREQ_SCALE * count_of(row + 1), own_rate),
-    )
-    edge_rates = [edge_rate * float(n) for n in range(1, harmonics + 1)]
-    next_rates = [next_rate * float(n) for n in range(1, harmonics + 1)]
-
     fetch.wait()
     fetch_in.wait()
 
@@ -306,6 +252,60 @@
     for c in range(comps):
         in_edge[c] = place(in_main[c], 1)
 
+    fetch_modes.wait()
+    fetch_counts.wait()
+    sign = jnp.where((sub // 2) % 2 == 0, 1.0, -1.0).astype(jnp.float32)
+
+    def mode_of(interface, n):
+        value = jnp.int32(0)
+        for i in range(rows_total - 1):
+            value = value + jnp.where(interface == i, modes[i, n], 0)
+        return value
+
+    def count_of(wanted):
+        value = jnp.int32(0)
+        for i in range(rows_total):
+            value = value + jnp.where(wanted == i, counts[i], 0)
+        return value.astype(jnp.float32)
+
+    def tables(modes_at, columns):
+        made = []
+        for n in range(harmonics):
+            product = modes_at(n) * columns
+            if total_columns & (total_columns - 1) == 0:
+                turns = product & (total_columns - 1)
+            else:
+                turns = jnp.remainder(product, total_columns)
+            angle = (2.0 * math.pi / total_columns) * turns.astype(jnp.float32)
+            made.append((jnp.cos(angle), jnp.sin(angle)))
+        return made
+
+    tab_main = [
+        (cosine, sign * sine)
+        for cosine, sine in tables(
+            lambda n: jnp.where(sub < 4, mode_of(row - 1, n), mode_of(row, n)), blk * width + lane
+        )
+    ]
+    edge_column = jnp.where(off < 3 * HALO, off - HALO, off + width - 5 * HALO)
+
+    def edge_mode(n):
+        lower, upper = mode_of(row - 1, n), mode_of(row, n)
+        rising = jnp.where(part == 0, lower, jnp.where(part == layers, upper, 0))
+        falling = jnp.where(part == 1, -lower, jnp.where(part == layers + 1, -upper, 0))
+        return jnp.where(sub < 4, falling, rising)
+
+    tab_edge = tables(edge_mode, blk * width + edge_column)
+    own_rate = FREQ_SCALE * count_of(row)
+    next_rate = jnp.where(sub < 4, FREQ_SCALE * count_of(row - 1), FREQ_SCALE * count_of(row + 1))
+    own_rates = [own_rate * float(n) for n in range(1, harmonics + 1)]
+    edge_rate = jnp.where(
+        part == 0,
+        FREQ_SCALE * count_of(row - 1),
+        jnp.where(part == layers + 1, FREQ_SCALE * count_of(row + 1), own_rate),
+    )
+    edge_rates = [edge_rate * float(n) for n in range(1, harmonics + 1)]
+    next_rates = [next_rate * float(n) for n in range(1, harmonics + 1)]
+
     @pl.when(has_low)
     def _():
         up[2].wait_recv()
@@ -355,7 +355,7 @@
                 save(imag_at, real * sine + imag * cosine)
             return carry
 
-        lax.fori_loop(0, nvars, per_var, 0)
+        lax.fori_loop(0, nvars, per_var, 0, unroll=True)
 
     def both(e, f, x, y, inflow_of, table, emit):
         x[:, 4:6, :] = e[:, PAD : PAD + 2, :]

time: 15.2 us -> 13.5 us (0.89)
  Pallas kernels: 14.3 us -> 12.6 us
    pallas_call x1, Pallas kernels: 14.3 us -> 12.6 us  [body(): pl.pallas_call(functools.partial(kernel, rows_total, blocks, nvars), out_...]
where the time goes in v4:
time: 13.5 us; the launch traced here: 13.4 us
  Pallas kernels  12.6 us (93%)
  local copies, waits for them, and re-layouts  0.74 us (5%)
    pallas_call x1, Pallas kernels, body(): pl.pallas_call(functools.partial(kernel, rows_total, blocks, nvars), out_...  12.6 us
    unnamed x1, local copies, waits for them, and re-layouts  0.74 us

profile of v4, /device:TPU:0, one launch (start us, length us, event | category | flops | bytes accessed | tf_op | source)
XLA Modules:
  0.0 13.4 jit_solution(10411619232469804839)
XLA Ops:
  0.0 12.6 %shard_map.46 = f32[45,16,128]{2,1,0:T(8,128)S(1)} custom-call(s32[1,4]{1,0:T(1,128)} %modes_in.1, s32[2]{0:T(128)} %counts_in.1, f32[45,16,128]{2,1,0:T(8,128)} %bitcast.3, f32[9,5,128]{2,1,0:T(8,128)} %inflow.1), custom_call_target="tpu_custom_call" | custom-call | tf_op jit(solution)/shard_map/pallas_call | solution.py:522
  12.7 0.7 %copy.6 = f32[1,9,5,16,128]{4,3,2,1,0:T(8,128)} copy(f32[1,9,5,16,128]{4,3,2,1,0:T(8,128)S(1)} %bitcast.2) | data formatting | bytes 737280
